TPU v7x, 512 devices: a whole 4x8x8 slice. The times are simulated.
512 devices in a mesh: req: 8 (over y), seq: 8 (over x, core), tp: 8 (over z).
Axes of the slice: x: 4, y: 8, z: 8, core: 2. Of those that a mesh axis runs over, the one named last changes fastest.
Arguments:
- tokens: bfloat16 [2048, 1024], P(('req', 'seq', 'tp')), may hold values from -3 to 3
- w_qkv: bfloat16 [1024, 3, 1024], P(None, None, 'tp'), may hold values from -0.1875 to 0.1875
- w_out: bfloat16 [1024, 1024], P('tp'), may hold values from -0.75 to 0.75
- variate_bias: float32 [2, 16], P(None, 'tp'), may hold values from -2 to 2
- attn_gain: float32 [1024], replicated, may hold values from 0.25 to 1.75
- ffn_gain: float32 [1024], replicated, may hold values from 0.25 to 1.75
- gate_up: bfloat16 [1024, 64, 128], P(None, ('seq', 'tp')), may hold values from -0.1875 to 0.1875
- w_down: bfloat16 [64, 64, 1024], P(('seq', 'tp')), may hold values from -0.09375 to 0.09375
- cache_keys: bfloat16 [1536, 256, 1024], P(('req', 'seq'), None, 'tp'), may hold values from -360 to 360
- cache_values: bfloat16 [1536, 256, 1024], P(('req', 'seq'), None, 'tp'), may hold values from -6 to 6
- cache_variate: int32 [1536, 256], P(('req', 'seq')), may hold values from 0 to 3
- new_variate: int32 [512, 4], P('req'), may hold values from 0 to 3
- piece_slot: int32 [512, 64], P('req'), may hold values from -1 to 191, as said below
- cache_len: int32 [512], P('req'), may hold values from 1 to 16384, as said below
Outputs:
- layer_out: bfloat16 [2048, 1024], P(('req', 'seq', 'tp'))
Inputs may be any that keep to these rules, and one draw needn't show every extreme that they name: `cache_len`: in each aligned block of 64 requests exactly one request has the most cached positions. `piece_slot`: entry p of request r is the slot within its group that holds cache positions p * 256 to p * 256 + 255; it is -1 exactly when p * 256 >= cache_len[r]; no slot of a group holds two pieces; slots that hold no piece are never read.
All inputs are finite; a program needn't handle non-finite values.
Results may differ from a plain program's by a relative error of at most 0.022.
Values may be sent and summed in bfloat16 or wider, within the bound.
No kernel may reach another device: no remote copies, remote signals or barrier semaphores. Data moves between devices by JAX's collectives and lax.ppermute only.
A program may use at most 64 MiB of HBM per device.

v0:
```python
import math
import jax
import jax.numpy as jnp
from jax import lax
from jax.sharding import PartitionSpec as P

HD = 64
EPSILON = 1e-05
MASKED_SCORE = -1e30


def joined(value, axis, combine):
    everything = jax.tree.map(lambda part: lax.all_gather(part, axis), value)
    first = jax.tree.map(lambda part: part[0], everything)

    def step(k, so_far):
        return combine(so_far, jax.tree.map(lambda part: part[k], everything))

    return lax.fori_loop(1, lax.axis_size(axis), step, first)


def rms_scale(rows, gain):
    rows32 = rows.astype(jnp.float32)
    mean_sq = jnp.mean(rows32 * rows32, axis=-1, keepdims=True)
    return (rows32 * lax.rsqrt(mean_sq + EPSILON) * gain).astype(jnp.bfloat16)


def rotate(vectors, positions):
    half_size = vectors.shape[-1] // 2
    inv_freq = 10000.0 ** (-jnp.arange(half_size, dtype=jnp.float32) / half_size)
    angles = positions[:, None] * inv_freq[None, :]
    cosine = jnp.cos(angles)[:, None, :]
    sine_part = jnp.sin(angles)[:, None, :]
    earlier = vectors[..., :half_size]
    latter = vectors[..., half_size:]
    return jnp.concatenate(
        [earlier * cosine - latter * sine_part, latter * cosine + earlier * sine_part], axis=-1
    )


def row_positions(lengths, step_count):
    offsets = jnp.arange(step_count, dtype=jnp.int32)
    return (lengths[:, None] + offsets[None, :]).reshape(-1).astype(jnp.float32)


def split_heads(projected, positions, head_size):
    row_count = projected.shape[0]
    parts = projected.reshape(row_count, 3, -1, head_size)
    queries = rotate(parts[:, 0], positions).astype(jnp.bfloat16)
    keys_new = rotate(parts[:, 1], positions).astype(jnp.bfloat16)
    values_new = parts[:, 2].astype(jnp.bfloat16)
    return (queries, keys_new, values_new)


def cache_partials(
    queries,
    cache_keys,
    cache_values,
    cache_variate,
    new_variate,
    piece_slot,
    cache_len,
    variate_bias,
    score_scale,
):
    slot_count, piece_len, _ = cache_keys.shape
    requests, step_count, heads, head_size = queries.shape
    max_pieces = piece_slot.shape[1]
    slot_ids = lax.axis_index("seq") * slot_count + jnp.arange(slot_count, dtype=jnp.int32)
    matches = piece_slot[None, :, :] == slot_ids[:, None, None]
    owners = jnp.any(matches, axis=2)
    piece_index = jnp.sum(
        jnp.where(matches, jnp.arange(max_pieces, dtype=jnp.int32)[None, None, :], 0), axis=(1, 2)
    )
    owner_len = jnp.sum(jnp.where(owners, cache_len[None, :], 0), axis=1)
    positions_in = (
        piece_index[:, None] * piece_len + jnp.arange(piece_len, dtype=jnp.int32)[None, :]
    )
    is_valid = positions_in < owner_len[:, None]
    picker = owners.astype(jnp.bfloat16)
    slot_query = jnp.dot(
        picker, queries.reshape(requests, -1), preferred_element_type=jnp.float32
    ).astype(jnp.bfloat16)
    slot_query = slot_query.reshape(slot_count, step_count, heads, head_size)
    slot_variate = jnp.sum(jnp.where(owners[:, :, None], new_variate[None], 0), axis=1)
    same_var = slot_variate[:, :, None] == cache_variate[:, None, :]
    bias_terms = jnp.where(
        same_var[:, None],
        variate_bias[0][None, :, None, None],
        variate_bias[1][None, :, None, None],
    )
    key_rows = cache_keys.reshape(slot_count, piece_len, heads, head_size)
    value_rows = cache_values.reshape(slot_count, piece_len, heads, head_size)
    scores = (
        jnp.einsum("sthd,slhd->shtl", slot_query, key_rows, preferred_element_type=jnp.float32)
        * score_scale
        + bias_terms
    )
    scores = jnp.where(is_valid[:, None, None, :], scores, MASKED_SCORE)
    slot_top = jnp.max(scores, axis=3)
    weights = jnp.where(is_valid[:, None, None, :], jnp.exp(scores - slot_top[..., None]), 0.0)
    slot_total = jnp.sum(weights, axis=3)
    slot_out = jnp.einsum(
        "shtl,slhd->shtd",
        weights.astype(jnp.bfloat16),
        value_rows,
        preferred_element_type=jnp.float32,
    )
    top_cache = jnp.max(
        jnp.where(owners[:, :, None, None], slot_top[:, None], MASKED_SCORE), axis=0
    )
    top_at = jnp.sum(jnp.where(owners[:, :, None, None], top_cache[None], 0.0), axis=1)
    factor = jnp.exp(slot_top - top_at)
    owner_f = owners.astype(jnp.float32)
    cache_total = jnp.einsum(
        "sr,sht->rht", owner_f, slot_total * factor, precision=lax.Precision.HIGHEST
    )
    cache_out = jnp.einsum(
        "sr,shtd->rhtd", owner_f, slot_out * factor[..., None], precision=lax.Precision.HIGHEST
    )
    return (top_cache, cache_total, cache_out)


def merge_pair(earlier, latter):
    joint_top = jnp.maximum(earlier[0], latter[0])
    left_scale = jnp.exp(earlier[0] - joint_top)
    right_scale = jnp.exp(latter[0] - joint_top)
    joint_total = earlier[1] * left_scale + latter[1] * right_scale
    joint_out = earlier[2] * left_scale[..., None] + latter[2] * right_scale[..., None]
    return (joint_top, joint_total, joint_out)


def finish(
    top_cache,
    cache_total,
    cache_out,
    queries,
    keys_new,
    values_new,
    new_variate,
    variate_bias,
    score_scale,
):
    step_count = new_variate.shape[1]
    new_scores = (
        jnp.einsum("rthd,ruhd->rhtu", queries, keys_new, preferred_element_type=jnp.float32)
        * score_scale
    )
    same_var = new_variate[:, :, None] == new_variate[:, None, :]
    new_scores = new_scores + jnp.where(
        same_var[:, None],
        variate_bias[0][None, :, None, None],
        variate_bias[1][None, :, None, None],
    )
    step_ids = jnp.arange(step_count, dtype=jnp.int32)
    causal = step_ids[:, None] >= step_ids[None, :]
    new_scores = jnp.where(causal[None, None], new_scores, MASKED_SCORE)
    row_top = jnp.maximum(top_cache, jnp.max(new_scores, axis=3))
    new_weights = jnp.where(causal[None, None], jnp.exp(new_scores - row_top[..., None]), 0.0)
    carried = jnp.exp(top_cache - row_top)
    row_total = cache_total * carried + jnp.sum(new_weights, axis=3)
    mixed_out = cache_out * carried[..., None] + jnp.einsum(
        "rhtu,ruhd->rhtd",
        new_weights.astype(jnp.bfloat16),
        values_new,
        preferred_element_type=jnp.float32,
    )
    attended = mixed_out / row_total[..., None]
    requests, heads, _, head_size = attended.shape
    return (
        jnp.transpose(attended, (0, 2, 1, 3))
        .reshape(requests * step_count, heads * head_size)
        .astype(jnp.bfloat16)
    )


def make_expand(gate_blocks, unit_block, row_block):
    block_count = gate_blocks.shape[1]
    expanded = jnp.einsum("nd,dbu->nbu", row_block, gate_blocks, preferred_element_type=jnp.float32)
    gate_part = expanded[:, :, :unit_block]
    up_part = expanded[:, :, unit_block:]
    return (
        (jax.nn.silu(gate_part) * up_part)
        .astype(jnp.bfloat16)
        .reshape(row_block.shape[0], block_count * unit_block)
    )


def on_device(
    tokens,
    w_qkv,
    w_out,
    variate_bias,
    attn_gain,
    ffn_gain,
    gate_up,
    w_down,
    cache_keys,
    cache_values,
    cache_variate,
    new_variate,
    piece_slot,
    cache_len,
):
    row_count = tokens.shape[0]
    requests, step_count = new_variate.shape
    score_scale = 1.0 / math.sqrt(HD)
    normed = rms_scale(tokens, attn_gain)
    qkv_width = w_qkv.shape[2]
    flat_qkv = w_qkv.reshape(w_qkv.shape[0], 3 * qkv_width)
    projected = jnp.dot(
        lax.all_gather(normed, ("seq", "tp"), axis=0, tiled=True),
        flat_qkv,
        preferred_element_type=jnp.float32,
    )
    queries, keys_new, values_new = split_heads(projected, row_positions(cache_len, step_count), HD)
    shape_four = (requests, step_count, qkv_width // HD, HD)
    queries = queries.reshape(shape_four)
    keys_new = keys_new.reshape(shape_four)
    values_new = values_new.reshape(shape_four)
    top_cache, cache_total, cache_out = cache_partials(
        queries,
        cache_keys,
        cache_values,
        cache_variate,
        new_variate,
        piece_slot,
        cache_len,
        variate_bias,
        score_scale,
    )
    top_cache, cache_total, cache_out = joined(
        (top_cache, cache_total, cache_out), "seq", merge_pair
    )
    attended = finish(
        top_cache,
        cache_total,
        cache_out,
        queries,
        keys_new,
        values_new,
        new_variate,
        variate_bias,
        score_scale,
    )
    seq_base = lax.axis_index("seq") * (row_count * lax.axis_size("tp"))
    picked = lax.dynamic_slice_in_dim(attended, seq_base, row_count * lax.axis_size("tp"), 0)
    attn_rows_sum = lax.psum_scatter(
        jnp.dot(picked, w_out, preferred_element_type=jnp.float32).astype(jnp.bfloat16),
        "tp",
        scatter_dimension=0,
        tiled=True,
    ).astype(jnp.float32)
    mid = tokens.astype(jnp.float32) + attn_rows_sum
    normed_mid = rms_scale(mid, ffn_gain)
    unit_block = w_down.shape[1]
    model_width = w_down.shape[2]
    hidden = make_expand(
        gate_up, unit_block, lax.all_gather(normed_mid, ("seq", "tp"), axis=0, tiled=True)
    )
    flat_down = w_down.reshape(w_down.shape[0] * unit_block, model_width)
    picked = hidden
    ffn_rows_sum = lax.psum_scatter(
        jnp.dot(picked, flat_down, preferred_element_type=jnp.float32),
        ("seq", "tp"),
        scatter_dimension=0,
        tiled=True,
    )
    return (mid + ffn_rows_sum).astype(jnp.bfloat16)


def solution(mesh):
    in_specs = (
        P(("req", "seq", "tp"), None),
        P(None, None, "tp"),
        P("tp", None),
        P(None, "tp"),
        P(),
        P(),
        P(None, ("seq", "tp"), None),
        P(("seq", "tp"), None, None),
        P(("req", "seq"), None, "tp"),
        P(("req", "seq"), None, "tp"),
        P(("req", "seq"), None),
        P("req", None),
        P("req", None),
        P("req"),
    )
    out_specs = P(("req", "seq", "tp"), None)
    return jax.shard_map(
        on_device, mesh=mesh, in_specs=in_specs, out_specs=out_specs, check_vma=False
    )
```

profile of v0, /device:TPU:8, one launch (start us, length us, event | category | flops | bytes accessed | tf_op | source)
XLA Modules:
  0.0 463.1 jit_solution(17933760203444792327)
XLA Ops:
  6.6 1.4 fusion.9
  8.0 1.3 compare_reduce_fusion
  10.8 1.3 slice_bitcast_fusion.3
  12.8 1.3 select_reduce_fusion.3
  16.5 55.1 %all-gather.3 = bf16[64,4,1024]{2,1,0:T(4,128)(2,1)S(1)} all-gather(bf16[1,4,1024]{2,1,0:T(4,128)(2,1)S(1)} %fusion.39), channel_id=1, replica_groups=mesh['req'=8,'seq'=8,'tp'=8] {'seq','tp'}, dimensions={0}, use_global_device_ids=true | all-gather | bytes 532480 | tf_op jit(solution)/shard_map/all_gather | solution.py:212
  76.4 1.7 fusion.47
  78.3 1.2 fusion.20
  80.5 1.5 convolution_multiply_fusion.1
  82.0 1.0 fusion.22
  85.9 13.5 %all-gather = f32[512,2,4]{2,1,0:T(2,128)S(1)} all-gather(f32[64,2,4]{2,1,0:T(2,128)S(1)} %copy.150), channel_id=2, replica_groups=mesh['req'=8,'seq'=8,'tp'=8] {'seq'}, dimensions={0}, use_global_device_ids=true | all-gather | bytes 18432 | tf_op jit(solution)/shard_map/all_gather | solution.py:13
  99.7 13.6 %all-gather.1 = f32[512,2,4]{2,1,0:T(2,128)S(1)} all-gather(f32[64,2,4]{2,1,0:T(2,128)S(1)} %copy.153), channel_id=3, replica_groups=mesh['req'=8,'seq'=8,'tp'=8] {'seq'}, dimensions={0}, use_global_device_ids=true | all-gather | bytes 18432 | tf_op jit(solution)/shard_map/all_gather | solution.py:13
  114.9 14.4 %while.19 = (s32[]{:T(128)}, f32[64,2,4]{0,2,1:T(4,128)S(1)}, f32[64,2,4]{0,2,1:T(4,128)S(1)}, f32[64,2,4,64]{3,2,1,0:T(4,128)S(1)}, f32[8,64,2,4]{1,3,2,0:T(4,1...) while((s32[]{:T(128)}, f32[64,2,4]{0,2,1:T(4,128)S(1)}, ...), condition=%wide.region_10.11_spmd, body=%wide.region_9.10_spmd.sunk | while | flops 101381 | bytes 684175 | solution.py:19
  115.2 1.0 constant_dynamic-slice_fusion.2
  117.3 1.0 constant_dynamic-slice_fusion.2
  119.4 1.0 constant_dynamic-slice_fusion.2
  123.5 1.0 constant_dynamic-slice_fusion.2
  125.5 1.0 constant_dynamic-slice_fusion.2
  131.5 1.3 dynamic-slice
  133.4 74.0 %all-reduce.5.cloned.1.call-done = bf16[32,1024]{1,0:T(8,128)(2,1)} async-done(((bf16[32,1024]{1,0:T(8,128)(2,1)}), bf16[32,1024]{1,0:T(8,128)(2,1)}) %all-reduce.5.cloned.1.call-update) | async-done | bytes 65552
  209.0 48.0 %all-gather.4 = bf16[64,4,1024]{2,1,0:T(4,128)(2,1)S(1)} all-gather(bf16[1,4,1024]{2,1,0:T(4,128)(2,1)S(1)} %fusion.38), channel_id=1, replica_groups=mesh['req'=8,'seq'=8,'tp'=8] {'seq','tp'}, dimensions={0}, use_global_device_ids=true | all-gather | bytes 532480 | tf_op jit(solution)/shard_map/all_gather | solution.py:259
  257.5 1.4 fusion.13
  258.9 1.3 dynamic-slice.2
  260.8 194.3 %all-reduce.7.cloned.1.call-done = f32[256,1024]{1,0:T(8,128)} async-done(((f32[256,1024]{1,0:T(8,128)}), f32[256,1024]{1,0:T(8,128)}) %all-reduce.7.cloned.1.call-update) | async-done | bytes 1048592
  455.2 1.4 fusion.34
  (142 shorter events, 28.5 us)
Async XLA Ops:
  6.5 124.0 %copy-start = (bf16[128,1024]{1,0:T(8,128)(2,1)S(1)}, bf16[128,1024]{1,0:T(8,128)(2,1)}, u32[]{:S(2)}) copy-start(bf16[128,1024]{1,0:T(8,128)(2,1)} %param.18) | copy-start | bytes 786436
  6.5 65.1 %copy-start.4 = (bf16[1024,3,128]{2,0,1:T(8,128)(2,1)S(1)}, bf16[1024,3,128]{2,0,1:T(8,128)(2,1)}, u32[]{:S(2)}) copy-start(bf16[1024,3,128]{2,0,1:T(8,128)(2,1)} %param.17) | copy-start | bytes 2359300
  6.5 107.2 %all-gather.7.cloned.1.call-start = ((), (), s32[]{:S(2)}) async-start(), calls=%async_computation | async-start | bytes 2359296 | tf_op jit(solution)/shard_map/all_gather | solution.py:13
  72.0 2.6 copy-start.1
  72.4 0.8 copy-start.3
  74.5 0.7 copy-start.16
  74.6 0.7 copy-start.17
  74.6 0.8 copy-start.12
  75.3 4.4 copy-start.2
  75.4 2.6 copy-start.10
  79.7 0.7 copy-start.11
  80.5 4.1 copy-start.8
  80.5 4.2 copy-start.7
  83.1 124.3 %all-reduce.5.cloned.1.call-start = ((), (), s32[]{:S(2)}) async-start(), calls=%async_computation.1 | async-start | bytes 131072
  85.5 28.2 %copy-start.13 = (s32[64,4]{0,1:T(4,128)S(1)}, s32[64,4]{0,1:T(4,128)}, u32[]{:S(2)}) copy-start(s32[64,4]{0,1:T(4,128)} %param.27) | copy-start | bytes 3076
  85.5 28.2 %copy-start.14 = (f32[2]{0:T(128)S(1)}, f32[2]{0:T(128)}, u32[]{:S(2)}) copy-start(f32[2]{0:T(128)} %get-tuple-element.258) | copy-start | bytes 28
  129.9 77.5 %copy-start.6 = (bf16[4,1024]{1,0:T(4,128)(2,1)S(1)}, bf16[4,1024]{1,0:T(4,128)(2,1)}, u32[]{:S(2)}) copy-start(bf16[4,1024]{1,0:T(4,128)(2,1)} %param.16) | copy-start | bytes 24580
  129.9 78.3 %copy-start.15 = (f32[1024]{0:T(1024)S(1)}, f32[1024]{0:T(1024)}, u32[]{:S(2)}) copy-start(f32[1024]{0:T(1024)} %param.21) | copy-start | bytes 12292
  130.3 126.9 %copy-start.5 = (bf16[1024,1,128]{2,0,1:T(8,128)(2,1)S(1)}, bf16[1024,1,128]{2,0,1:T(8,128)(2,1)}, u32[]{:S(2)}) copy-start(bf16[1024,1,128]{2,0,1:T(8,128)(2,1)} %param.22) | copy-start | bytes 786436
  130.4 127.1 %copy-start.9 = (bf16[1,64,1024]{2,1,0:T(8,128)(2,1)S(1)}, bf16[1,64,1024]{2,1,0:T(8,128)(2,1)}, u32[]{:S(2)}) copy-start(bf16[1,64,1024]{2,1,0:T(8,128)(2,1)} %param.23) | copy-start | bytes 393220
  131.4 323.8 %all-reduce.7.cloned.1.call-start = ((), (), s32[]{:S(2)}) async-start(), calls=%async_computation.2 | async-start | bytes 2097152
Sparse Core Ops, SparseCore 0:
  83.2 27.9 all-gather.6
  131.5 75.8 all-reduce.4
  259.0 196.1 all-reduce.6
where the time goes:
time: 464 us; the launch traced here: 463 us
  waiting for transfers between devices  268 us (58%)
  blocking collectives  130 us (28%)
  local copies, waits for them, and re-layouts  20.9 us (5%)
  other arithmetic  20.4 us (4%)
  between operations  14.9 us (3%)
  matrix products  7.98 us (2%)
    unnamed x5, waiting for transfers between devices  268 us
    all_gather x1, blocking collectives, on_device(): lax.all_gather(normed, ('seq', 'tp'), axis=0, tiled=True)  55.1 us
    all_gather x1, blocking collectives, on_device(): lax.all_gather(normed_mid, ('seq', 'tp'), axis=0, tiled=True)  48 us
    all_gather x2, blocking collectives, joined(): everything = jax.tree.map(lambda part: lax.all_gather(part, axis), value)  27.1 us
  transfers between devices with their start and end apart: 3, of which 2 were waited for; matrix products, arithmetic and copies ran while one was open for 1% of the time, Pallas kernels for 0%

commit v1 on v0

--- a/solution.py
+++ b/solution.py
@@ -208,11 +208,15 @@
     normed = rms_scale(tokens, attn_gain)
     qkv_width = w_qkv.shape[2]
     flat_qkv = w_qkv.reshape(w_qkv.shape[0], 3 * qkv_width)
-    projected = jnp.dot(
-        lax.all_gather(normed, ("seq", "tp"), axis=0, tiled=True),
-        flat_qkv,
-        preferred_element_type=jnp.float32,
-    )
+
+    def try_all_roots(where_dim, in_array):
+        mixed_arr = lax.psum(1, axis_name=("seq", "tp"))
+        x_new = jnp.concatenate(mixed_arr * [in_array], where_dim)
+        return lax.all_to_all(
+            x_new, axis_name=("seq", "tp"), split_axis=where_dim, concat_axis=where_dim, tiled=True
+        )
+
+    projected = jnp.dot(try_all_roots(0, normed), flat_qkv, preferred_element_type=jnp.float32)
     queries, keys_new, values_new = split_heads(projected, row_positions(cache_len, step_count), HD)
     shape_four = (requests, step_count, qkv_width // HD, HD)
     queries = queries.reshape(shape_four)

time: 464 us -> 437 us (0.942)
  blocking collectives: 130 us -> 75.2 us
  starting transfers between devices: 0.09 us -> 13.9 us
  waiting for transfers between devices: 268 us -> 278 us
  local copies, waits for them, and re-layouts: 20.9 us -> 27.3 us
    all_gather x1 -> x0, blocking collectives: 55.1 us -> none  [on_device(): lax.all_gather(normed, ('seq', 'tp'), axis=0, tiled=True)]
    all_to_all x0 -> x1, starting transfers between devices: none -> 13.8 us  [try_all_roots(): lax.all_to_all(x_new, axis_name=('seq', 'tp'), split_axis=where_dim, conc...]
    all_to_all x0 -> x1, waiting for transfers between devices: none -> 10 us  [try_all_roots(): lax.all_to_all(x_new, axis_name=('seq', 'tp'), split_axis=where_dim, conc...]
  transfers between devices with their start and end apart: 3 -> 4, of which waited for: 2 -> 3; matrix products, arithmetic and copies ran while one was open for 1% -> 3% of each run, Pallas kernels for 0% -> 0%
where the time goes in v1:
time: 437 us; the launch traced here: 436 us
  waiting for transfers between devices  278 us (64%)
  blocking collectives  75.2 us (17%)
  local copies, waits for them, and re-layouts  27.3 us (6%)
  other arithmetic  16.2 us (4%)
  between operations  14.9 us (3%)
  starting transfers between devices  13.9 us (3%)
  matrix products  9.99 us (2%)
    unnamed x5, waiting for transfers between devices  268 us
    all_gather x1, blocking collectives, on_device(): lax.all_gather(normed_mid, ('seq', 'tp'), axis=0, tiled=True)  48 us
    all_gather x2, blocking collectives, joined(): everything = jax.tree.map(lambda part: lax.all_gather(part, axis), value)  27.2 us
    all_to_all x1, starting transfers between devices, try_all_roots(): lax.all_to_all(x_new, axis_name=('seq', 'tp'), split_axis=where_dim, conc...  13.8 us
    all_to_all x1, waiting for transfers between devices, try_all_roots(): lax.all_to_all(x_new, axis_name=('seq', 'tp'), split_axis=where_dim, conc...  10 us
  transfers between devices with their start and end apart: 4, of which 3 were waited for; matrix products, arithmetic and copies ran while one was open for 3% of the time, Pallas kernels for 0%

profile of v1, /device:TPU:8, one launch (start us, length us, event | category | flops | bytes accessed | tf_op | source)
XLA Modules:
  0.0 435.5 jit_solution(8810666644449950414)
XLA Ops:
  8.2 1.0 concatenate.24
  9.3 1.0 all_to_all.8
  10.3 13.8 %all-to-all-start = ((bf16[64,4,1024]{2,1,0:T(4,128)(2,1)}), bf16[64,4,1024]{2,1,0:T(4,128)(2,1)S(1)}, u32[]{:S(2)}, u32[]{:S(2)}) async-start(bf16[64,4,1024]{2,1,0:T(4,128)(2,1)} %all_to_all.8), calls=%async_computation | async-start | bytes 1048576 | tf_op jit(solution)/shard_map/all_to_all | solution.py:215
  26.1 1.7 copy.146
  27.8 2.6 copy.154
  32.1 10.0 %all-to-all-done = bf16[64,4,1024]{2,1,0:T(4,128)(2,1)S(1)} async-done(((bf16[64,4,1024]{2,1,0:T(4,128)(2,1)}), bf16[64,4,1024]{2,1,0:T(4,128)(2,1)S(1)}, u32[]{:S(2)}, u32[]{:S(2)}) %all-to-all-start) | async-done | bytes 524320 | tf_op jit(solution)/shard_map/all_to_all | solution.py:215
  43.0 1.4 fusion.10
  49.9 1.8 fusion.46
  52.1 1.2 fusion.20
  53.5 1.5 convolution_multiply_fusion.1
  55.0 1.0 fusion.22
  58.9 13.4 %all-gather = f32[512,2,4]{2,1,0:T(2,128)S(1)} all-gather(f32[64,2,4]{2,1,0:T(2,128)S(1)} %copy.150), channel_id=2, replica_groups=mesh['req'=8,'seq'=8,'tp'=8] {'seq'}, dimensions={0}, use_global_device_ids=true | all-gather | bytes 18432 | tf_op jit(solution)/shard_map/all_gather | solution.py:13
  72.7 13.7 %all-gather.1 = f32[512,2,4]{2,1,0:T(2,128)S(1)} all-gather(f32[64,2,4]{2,1,0:T(2,128)S(1)} %copy.153), channel_id=3, replica_groups=mesh['req'=8,'seq'=8,'tp'=8] {'seq'}, dimensions={0}, use_global_device_ids=true | all-gather | bytes 18432 | tf_op jit(solution)/shard_map/all_gather | solution.py:13
  88.1 14.4 %while.19 = (s32[]{:T(128)}, f32[64,2,4]{0,2,1:T(4,128)S(1)}, f32[64,2,4]{0,2,1:T(4,128)S(1)}, f32[64,2,4,64]{3,2,1,0:T(4,128)S(1)}, f32[8,64,2,4]{1,3,2,0:T(4,1...) while((s32[]{:T(128)}, f32[64,2,4]{0,2,1:T(4,128)S(1)}, ...), condition=%wide.region_10.11_spmd, body=%wide.region_9.10_spmd.sunk | while | flops 101381 | bytes 684175 | solution.py:19
  88.3 1.0 constant_dynamic-slice_fusion.2
  90.4 1.0 constant_dynamic-slice_fusion.2
  94.5 1.0 constant_dynamic-slice_fusion.2
  104.6 1.3 dynamic-slice
  106.5 73.2 %all-reduce.5.cloned.1.call-done = bf16[32,1024]{1,0:T(8,128)(2,1)} async-done(((bf16[32,1024]{1,0:T(8,128)(2,1)}), bf16[32,1024]{1,0:T(8,128)(2,1)}) %all-reduce.5.cloned.1.call-update) | async-done | bytes 65552
  181.3 48.0 %all-gather.3 = bf16[64,4,1024]{2,1,0:T(4,128)(2,1)S(1)} all-gather(bf16[1,4,1024]{2,1,0:T(4,128)(2,1)S(1)} %fusion.38), channel_id=1, replica_groups=mesh['req'=8,'seq'=8,'tp'=8] {'seq','tp'}, dimensions={0}, use_global_device_ids=true | all-gather | bytes 532480 | tf_op jit(solution)/shard_map/all_gather | solution.py:263
  229.8 1.4 fusion.13
  231.2 1.3 dynamic-slice.2
  233.1 194.5 %all-reduce.7.cloned.1.call-done = f32[256,1024]{1,0:T(8,128)} async-done(((f32[256,1024]{1,0:T(8,128)}), f32[256,1024]{1,0:T(8,128)}) %all-reduce.7.cloned.1.call-update) | async-done | bytes 1048592
  427.6 1.4 fusion.34
  (151 shorter events, 32.1 us)
Async XLA Ops:
  6.5 97.1 %copy-start = (bf16[128,1024]{1,0:T(8,128)(2,1)S(1)}, bf16[128,1024]{1,0:T(8,128)(2,1)}, u32[]{:S(2)}) copy-start(bf16[128,1024]{1,0:T(8,128)(2,1)} %param.18) | copy-start | bytes 786436
  8.2 15.9 %copy-start.13 = (s32[64,64]{1,0:T(8,128)S(1)}, s32[64,64]{1,0:T(8,128)}, u32[]{:S(2)}) copy-start(s32[64,64]{1,0:T(8,128)} %param.28) | copy-start | bytes 49156
  8.2 17.1 %copy-start.19 = (s32[64]{0:T(128)S(1)}, s32[64]{0:T(128)}, u32[]{:S(2)}) copy-start(s32[64]{0:T(128)} %param.29) | copy-start | bytes 772
  8.2 17.2 %copy-start.15 = (s32[64,4]{0,1:T(4,128)S(1)}, s32[64,4]{0,1:T(4,128)}, u32[]{:S(2)}) copy-start(s32[64,4]{0,1:T(4,128)} %param.27) | copy-start | bytes 3076
  8.2 17.5 %copy-start.3 = (bf16[1024,3,128]{2,0,1:T(8,128)(2,1)S(1)}, bf16[1024,3,128]{2,0,1:T(8,128)(2,1)}, u32[]{:S(2)}) copy-start(bf16[1024,3,128]{2,0,1:T(8,128)(2,1)} %param.17) | copy-start | bytes 2359300
  10.3 31.8 %all-to-all-start = ((bf16[64,4,1024]{2,1,0:T(4,128)(2,1)}), bf16[64,4,1024]{2,1,0:T(4,128)(2,1)S(1)}, u32[]{:S(2)}, u32[]{:S(2)}) async-start(bf16[64,4,1024]{2,1,0:T(4,128)(2,1)} %all_to_all.8), calls=%async_computation | async-start | bytes 1048576 | tf_op jit(solution)/shard_map/all_to_all | solution.py:215
  24.1 62.8 %all-gather.6.cloned.1.call-start = ((), (), s32[]{:S(2)}) async-start(), calls=%async_computation.1 | async-start | bytes 2359296 | tf_op jit(solution)/shard_map/all_gather | solution.py:13
  27.8 2.7 copy-start.20
  27.8 3.4 copy-start.14
  44.5 0.7 copy-start.2
  45.9 0.6 copy-start.6
  45.9 7.5 %copy-start.1 = (bf16[24,256,128]{1,2,0:T(8,128)(2,1)S(1)}, bf16[24,256,128]{1,2,0:T(8,128)(2,1)}, u32[]{:S(2)}) copy-start(bf16[24,256,128]{1,2,0:T(8,128)(2,1)} %copy.154) | copy-start | bytes 4718596
  53.5 3.6 copy-start.7
  53.5 3.7 copy-start.5
  53.5 4.1 copy-start.11
  53.5 4.2 copy-start.10
  56.1 123.6 %all-reduce.5.cloned.1.call-start = ((), (), s32[]{:S(2)}) async-start(), calls=%async_computation.2 | async-start | bytes 131072
  58.5 28.2 %copy-start.16 = (f32[2]{0:T(128)S(1)}, f32[2]{0:T(128)}, u32[]{:S(2)}) copy-start(f32[2]{0:T(128)} %get-tuple-element.257) | copy-start | bytes 28
  58.5 28.2 %copy-start.17 = (f32[2]{0:T(128)S(1)}, f32[2]{0:T(128)}, u32[]{:S(2)}) copy-start(f32[2]{0:T(128)} %get-tuple-element.258) | copy-start | bytes 28
  103.0 76.6 %copy-start.9 = (bf16[4,1024]{1,0:T(4,128)(2,1)S(1)}, bf16[4,1024]{1,0:T(4,128)(2,1)}, u32[]{:S(2)}) copy-start(bf16[4,1024]{1,0:T(4,128)(2,1)} %param.16) | copy-start | bytes 24580
  103.0 77.5 %copy-start.18 = (f32[1024]{0:T(1024)S(1)}, f32[1024]{0:T(1024)}, u32[]{:S(2)}) copy-start(f32[1024]{0:T(1024)} %param.21) | copy-start | bytes 12292
  103.4 126.0 %copy-start.8 = (bf16[1024,1,128]{2,0,1:T(8,128)(2,1)S(1)}, bf16[1024,1,128]{2,0,1:T(8,128)(2,1)}, u32[]{:S(2)}) copy-start(bf16[1024,1,128]{2,0,1:T(8,128)(2,1)} %param.22) | copy-start | bytes 786436
  103.5 126.2 %copy-start.12 = (bf16[1,64,1024]{2,1,0:T(8,128)(2,1)S(1)}, bf16[1,64,1024]{2,1,0:T(8,128)(2,1)}, u32[]{:S(2)}) copy-start(bf16[1,64,1024]{2,1,0:T(8,128)(2,1)} %param.23) | copy-start | bytes 393220
  104.5 323.1 %all-reduce.7.cloned.1.call-start = ((), (), s32[]{:S(2)}) async-start(), calls=%async_computation.3 | async-start | bytes 2097152
  (1 other events, 0.6 us)
Sparse Core Ops, SparseCore 0:
  56.2 27.3 all-gather.5
  104.6 74.9 all-reduce.4
  231.3 196.2 all-reduce.6
